TPU v7x, 32 devices: a whole 2x2x4 slice. The times are simulated.
32 devices in a mesh: segment: 2 (over x), rows: 8 (over z, y), cols: 2 (over core).
Axes of the slice: x: 2, y: 2, z: 4, core: 2. Of those that a mesh axis runs over, the one named last changes fastest.
Arguments:
- frames: bfloat16 [2, 2, 16, 128, 128], P(None, None, 'rows', 'cols'), may hold values from -6 to 6
- cell_weight: bfloat16 [9, 256, 512], P(None, 'rows'), may hold values from -0.125 to 0.125
- cell_bias: float32 [512], replicated, may hold values from -3 to 3
- first_context_weight: bfloat16 [9, 128, 384], P(None, 'rows'), may hold values from -1 to 1
- first_context_bias: float32 [384], replicated, may hold values from -0.5 to 1
- second_context_weight: bfloat16 [9, 384, 384], P(None, 'rows'), may hold values from -0.109375 to 0.109375
- second_context_bias: float32 [384], replicated, may hold values from -0.5 to 1
- third_context_weight: bfloat16 [9, 384, 384], P(None, 'rows'), may hold values from -0.109375 to 0.109375
- third_context_bias: float32 [384], replicated, may hold values from 0 to 1
Outputs:
- context: bfloat16 [2, 16, 128, 384], P('segment', 'rows', 'cols')
All inputs are finite; a program needn't handle non-finite values.
Results may differ from a plain program's by a relative error of at most 0.0065.
Values may be sent and summed in bfloat16 or wider, within the bound.
A program may use at most 64 MiB of HBM per device.

v0:
```python
import jax
import jax.numpy as jnp
from jax import lax
from jax.sharding import PartitionSpec as P

FIRST_DILATION = 16
SECOND_DILATION = 32
THIRD_DILATION = 64


def extended(value, sides, width):
    for axis, dim in sides:
        devices, length = (lax.axis_size(axis), value.shape[dim])
        up = [(i, (i + 1) % devices) for i in range(devices - 1)]
        down = [(j, i) for i, j in up]
        last = lax.slice_in_dim(value, length - width, length, axis=dim)
        leading = lax.slice_in_dim(value, 0, width, axis=dim)
        before = lax.ppermute(last, axis, up)
        after = lax.ppermute(leading, axis, down)
        value = jnp.concatenate([before, value, after], axis=dim)
    return value


def shortened(value):

    def short(part):
        return part.astype(jnp.bfloat16) if part.dtype == jnp.float32 else part

    return jax.tree.map(short, value)


def from_behind(value, axis, steps):
    count = lax.axis_size(axis)
    leading, last = (max(0, -steps), min(count, count - steps))
    return lax.ppermute(value, axis, [(source, source + steps) for source in range(leading, last)])


def tap_product(tap_list, weight):
    stacked = jnp.concatenate(tap_list, axis=-1)
    height, across, channels = stacked.shape
    flattened = stacked.reshape(height * across, channels)
    product = jnp.dot(
        flattened, weight.reshape(channels, weight.shape[-1]), preferred_element_type=jnp.float32
    )
    return product.reshape(height, across, weight.shape[-1])


def cell_update(padded, memory, weight, offset):
    height, across, channels = memory.shape
    tap_list = [
        padded[row_tap : row_tap + height, col_tap : col_tap + across]
        for row_tap in range(3)
        for col_tap in range(3)
    ]
    gate_sums = tap_product(tap_list, weight) + offset
    inflow = jax.nn.sigmoid(gate_sums[..., :channels])
    forget = jax.nn.sigmoid(gate_sums[..., channels : 2 * channels])
    output = jax.nn.sigmoid(gate_sums[..., 2 * channels : 3 * channels])
    update = jnp.tanh(gate_sums[..., 3 * channels :])
    memory = forget * memory + inflow * update
    hidden_state = (output * jnp.tanh(memory)).astype(jnp.bfloat16)
    return (hidden_state, memory)


def cell_section(clip, weight, offset, active_mask):
    height, across = (clip.shape[1], clip.shape[2])
    channels = offset.shape[0] // 4
    hidden_state = jnp.zeros((height, across, channels), jnp.bfloat16)
    memory = jnp.zeros((height, across, channels), jnp.float32)

    def cell_compute(operands):
        return cell_update(operands[0], operands[1], weight, offset)

    def cell_skipped(operands):
        return (jnp.zeros((height, across, channels), jnp.bfloat16), jnp.zeros_like(operands[1]))

    for moment in range(clip.shape[0]):
        joined = jnp.concatenate([clip[moment], hidden_state], axis=-1)
        padded = extended(joined, (("rows", 0), ("cols", 1)), 1)
        hidden_state, memory = lax.cond(active_mask, cell_compute, cell_skipped, (padded, memory))
    return hidden_state


def dilated_context_layer(feature, weight, offset, spacing, active_mask):
    height, across = (feature.shape[0], feature.shape[1])
    widened = extended(feature, (("cols", 1),), spacing)
    reach = spacing // height
    groups = lax.axis_size("rows")
    if reach >= groups:
        before = jnp.zeros_like(widened)
        beyond = jnp.zeros_like(widened)
    else:
        before = from_behind(shortened(widened), "rows", reach).astype(widened.dtype)
        beyond = from_behind(shortened(widened), "rows", -reach).astype(widened.dtype)
    row_taps = [before, widened, beyond]
    tap_list = [
        row_taps[row_tap][:, col_tap * spacing : col_tap * spacing + across]
        for row_tap in range(3)
        for col_tap in range(3)
    ]

    def dilated_compute(pieces):
        return jnp.maximum(tap_product(pieces, weight) + offset, 0.0)

    def dilated_skipped(pieces):
        return jnp.zeros((height, across, weight.shape[-1]), jnp.float32)

    return lax.cond(active_mask, dilated_compute, dilated_skipped, tap_list)


def context_section(hidden_state, kernel_list, offset_list, active_mask):
    first_output = dilated_context_layer(
        hidden_state, kernel_list[0], offset_list[0], FIRST_DILATION, active_mask
    ).astype(jnp.bfloat16)
    second_output = dilated_context_layer(
        first_output, kernel_list[1], offset_list[1], SECOND_DILATION, active_mask
    ).astype(jnp.bfloat16)
    third_output = dilated_context_layer(
        second_output, kernel_list[2], offset_list[2], THIRD_DILATION, active_mask
    )
    return (second_output.astype(jnp.float32) + third_output).astype(jnp.bfloat16)


def per_device(
    frames,
    cell_weight,
    cell_bias,
    first_context_weight,
    first_context_bias,
    second_context_weight,
    second_context_bias,
    third_context_weight,
    third_context_bias,
):
    full_cell, full_first, full_second, full_third = (
        lax.all_gather(cell_weight, "rows", axis=1, tiled=True),
        lax.all_gather(first_context_weight, "rows", axis=1, tiled=True),
        lax.all_gather(second_context_weight, "rows", axis=1, tiled=True),
        lax.all_gather(third_context_weight, "rows", axis=1, tiled=True),
    )
    kernel_list = (full_first, full_second, full_third)
    offset_list = (first_context_bias, second_context_bias, third_context_bias)
    segment_index = lax.axis_index("segment")
    micro_count = frames.shape[0]
    half_count = micro_count // 2
    always = jnp.array(True)
    own_frames = lax.dynamic_slice_in_dim(frames, segment_index * half_count, half_count, 0)
    state = cell_section(own_frames[0], full_cell, cell_bias, always)
    results = [context_section(state, kernel_list, offset_list, always)]
    return jnp.stack(results)


def solution(mesh):
    placed = (
        P(None, None, "rows", "cols", None),
        P(None, "rows", None),
        P(),
        P(None, "rows", None),
        P(),
        P(None, "rows", None),
        P(),
        P(None, "rows", None),
        P(),
    )
    return jax.shard_map(
        per_device,
        mesh=mesh,
        in_specs=placed,
        out_specs=P("segment", "rows", "cols", None),
        check_vma=False,
    )
```

profile of v0, /device:TPU:0, one launch (start us, length us, event | category | flops | bytes accessed | tf_op | source)
XLA Modules:
  0.0 190.7 jit_solution(9595188403604663498)
XLA Ops:
  8.9 4.9 %collective-permute-start = (bf16[1,64,256]{2,1,0:T(8,128)(2,1)S(1)}, bf16[1,64,256]{2,1,0:T(8,128)(2,1)S(1)}, u32[]{:S(2)}, u32[]{:S(2)}) collective-permute-start(bf16[1,64,256]{2,1,0:T(8,128)(2,1)S(1)} %get-tuple-element.23), channel_id=1, source_target_pairs={{0,2},{2,4},{4,6},{6,8},{8,10},{10,12},{12,14},{1,3},{3,5},{5,7},{... | collective-permute-start | bytes 98312 | tf_op jit(solution)/shard_map/ppermute | solution.py:18
  13.8 1.3 collective-permute-start.1
  15.1 36.8 %all_gather.13 = bf16[9,128,384]{2,1,0:T(8,128)(2,1)S(1)} all-gather(bf16[9,16,384]{2,1,0:T(8,128)(2,1)} %param.12), channel_id=1, replica_groups=mesh['segment'=2,'rows'=8,'cols'=2] {'rows'}, dimensions={1}, use_global_device_ids=true | all-gather | bytes 995328 | tf_op jit(solution)/shard_map/all_gather | solution.py:137
  53.3 1.3 collective-permute-start.3
  54.6 1.7 collective-permute-done.3
  56.6 12.3 %all-gather.4.cloned.1.call-done = bf16[9,256,512]{2,1,0:T(8,128)(2,1)} async-done(((bf16[9,32,512]{2,1,0:T(8,128)(2,1)}), bf16[9,256,512]{2,1,0:T(8,128)(2,1)}) %all-gather.4.cloned.1.call-update) | async-done | bytes 2359312 | tf_op jit(solution)/shard_map/all_gather | solution.py:136
  68.9 2.3 %convolution_add_fusion.1 = f32[2,64,512]{2,1,0:T(8,128)S(1)} fusion(bf16[2,64,2304]{2,1,0:T(8,128)(2,1)S(1)} %constant_dynamic-update-slice_fusion, bf16[2304,512,1]{1,0,2:T(8,128)(2,1)} %bitcast.28, f32[512]{0:T(512)S(1)} %copy-done.1), kind=kOutput, calls=%fused_computation.1 | convolution fusion | flops 302055424 | bytes 3213312 | tf_op jit(solution)/shard_map/cond/branch_1_fun/dot_general | solution.py:42
  71.3 3.4 %collective-permute-start.4 = (bf16[1,64,256]{2,1,0:T(8,128)(2,1)S(1)}, bf16[1,64,256]{2,1,0:T(8,128)(2,1)S(1)}, u32[]{:S(2)}, u32[]{:S(2)}) collective-permute-start(bf16[1,64,256]{2,1,0:T(8,128)(2,1)S(1)} %get-tuple-element.19), channel_id=1, source_target_pairs={{0,2},{2,4},{4,6},{6,8},{8,10},{10,12},{12,14},{1,3},{3,5},{5,7},{... | collective-permute-start | bytes 98312 | tf_op jit(solution)/shard_map/ppermute | solution.py:18
  74.7 1.3 collective-permute-start.5
  76.3 4.2 %collective-permute-done.5 = bf16[1,64,256]{2,1,0:T(8,128)(2,1)S(1)} collective-permute-done((bf16[1,64,256]{2,1,0:T(8,128)(2,1)S(1)}, bf16[1,64,256]{2,1,0:T(8,128)(2,1)S(1)}, u32[]{:S(2)}, u32[]{:S(2)}) %collective-permute-start.5) | collective-permute-done | bytes 32800 | tf_op jit(solution)/shard_map/ppermute | solution.py:19
  81.8 1.3 collective-permute-start.7
  83.1 1.7 collective-permute-done.7
  85.7 2.1 %collective-permute-start.8 = (bf16[2,16,128]{2,1,0:T(8,128)(2,1)S(1)}, bf16[2,16,128]{2,1,0:T(8,128)(2,1)S(1)}, u32[]{:S(2)}, u32[]{:S(2)}) collective-permute-start(bf16[2,16,128]{2,1,0:T(8,128)(2,1)S(1)} %get-tuple-element.22), channel_id=1, source_target_pairs={{0,1},{2,3},{4,5},{6,7},{8,9},{10,11},{12,13},{14,15},{16,17},{18,... | collective-permute-start | bytes 24584 | tf_op jit(solution)/shard_map/ppermute | solution.py:18
  87.8 1.3 collective-permute-start.9
  89.2 1.7 collective-permute-done.9
  91.3 2.1 %collective-permute-start.10 = (bf16[2,32,384]{2,1,0:T(8,128)(2,1)S(1)}, bf16[2,32,384]{2,1,0:T(8,128)(2,1)S(1)}, u32[]{:S(2)}, u32[]{:S(2)}) collective-permute-start(bf16[2,32,384]{2,1,0:T(8,128)(2,1)S(1)} %get-tuple-element.18), channel_id=1, source_target_pairs={{0,1},{2,3},{4,5},{6,7},{8,9},{10,11},{12,13},{14,15},{16,17},{18,... | collective-permute-start | bytes 147464 | tf_op jit(solution)/shard_map/ppermute | solution.py:18
  93.4 1.3 collective-permute-start.11
  94.8 1.8 collective-permute-done.11
  96.6 29.0 %all-gather.6.cloned.1.call-done = bf16[9,384,384]{2,1,0:T(8,128)(2,1)} async-done(((bf16[9,48,384]{2,1,0:T(8,128)(2,1)}), bf16[9,384,384]{2,1,0:T(8,128)(2,1)}) %all-gather.6.cloned.1.call-update) | async-done | bytes 2654224 | tf_op jit(solution)/shard_map/all_gather | solution.py:138
  125.5 2.4 %fusion.5 = bf16[2,64,384]{2,1,0:T(8,128)(2,1)S(1)} fusion(bf16[2,64,3456]{2,1,0:T(8,128)(2,1)S(1)} %constant_dynamic-update-slice_fusion.27, bf16[3456,384,1]{1,0,2:T(8,128)(2,1)} %bitcast.30, f32[384]{0:T(512)S(1)} %copy-done.3), kind=kOutput, calls=%fused_computation.10 | convolution fusion | flops 339886080 | bytes 3638784 | tf_op jit(solution)/shard_map/cond/branch_1_fun/dot_general | solution.py:42
  128.0 1.3 collective-permute-start.12
  130.6 1.8 collective-permute-done.13
  132.5 48.6 %all-gather.8.cloned.1.call-done = bf16[9,384,384]{2,1,0:T(8,128)(2,1)} async-done(((bf16[9,48,384]{2,1,0:T(8,128)(2,1)}), bf16[9,384,384]{2,1,0:T(8,128)(2,1)}) %all-gather.8.cloned.1.call-update) | async-done | bytes 2654224 | tf_op jit(solution)/shard_map/all_gather | solution.py:139
  181.2 3.0 %fusion.7 = bf16[1,2,64,384]{3,2,1,0:T(8,128)(2,1)} fusion(bf16[2,64,3456]{2,1,0:T(8,128)(2,1)S(1)} %constant_dynamic-update-slice_fusion.30, bf16[3456,384,1]{1,0,2:T(8,128)(2,1)} %bitcast.32, bf16[2,64,384]{2,1,0:T(8,128)(2,1)S(1)} %fusion.5, f32[384]{0:T(512)S(1)} %copy-done.2), kind=kOutput, calls=%fused_computation.12 | convolution fusion | flops 339984384 | bytes 3737088 | tf_op jit(solution)/shard_map/cond/branch_1_fun/dot_general | solution.py:42
  (82 shorter events, 8.2 us)
Async XLA Ops:
  6.5 62.3 %copy-start.1 = (f32[512]{0:T(512)S(1)}, f32[512]{0:T(512)}, u32[]{:S(2)}) copy-start(f32[512]{0:T(512)} %param.11) | copy-start | bytes 6148
  6.5 62.3 %all-gather.4.cloned.1.call-start = ((), (), s32[]{:S(2)}) async-start(), calls=%async_computation | async-start | bytes 2654208 | tf_op jit(solution)/shard_map/all_gather | solution.py:136
  7.3 118.3 %all-gather.6.cloned.1.call-start = ((), (), s32[]{:S(2)}) async-start(), calls=%async_computation.1 | async-start | bytes 2985984 | tf_op jit(solution)/shard_map/all_gather | solution.py:138
  8.0 173.2 %all-gather.8.cloned.1.call-start = ((), (), s32[]{:S(2)}) async-start(), calls=%async_computation.2 | async-start | bytes 2985984 | tf_op jit(solution)/shard_map/all_gather | solution.py:139
  8.9 43.1 %collective-permute-start = (bf16[1,64,256]{2,1,0:T(8,128)(2,1)S(1)}, bf16[1,64,256]{2,1,0:T(8,128)(2,1)S(1)}, u32[]{:S(2)}, u32[]{:S(2)}) collective-permute-start(bf16[1,64,256]{2,1,0:T(8,128)(2,1)S(1)} %get-tuple-element.23), channel_id=1, source_target_pairs={{0,2},{2,4},{4,6},{6,8},{8,10},{10,12},{12,14},{1,3},{3,5},{5,7},{... | collective-permute-start | bytes 98312 | tf_op jit(solution)/shard_map/ppermute | solution.py:18
  13.8 38.2 %collective-permute-start.1 = (bf16[1,64,256]{2,1,0:T(8,128)(2,1)S(1)}, bf16[1,64,256]{2,1,0:T(8,128)(2,1)S(1)}, u32[]{:S(2)}, u32[]{:S(2)}) collective-permute-start(bf16[1,64,256]{2,1,0:T(8,128)(2,1)S(1)} %get-tuple-element.24), channel_id=1, source_target_pairs={{2,0},{4,2},{6,4},{8,6},{10,8},{12,10},{14,12},{3,1},{5,3},{7,5},{... | collective-permute-start | bytes 98312 | tf_op jit(solution)/shard_map/ppermute | solution.py:19
  52.0 2.6 %collective-permute-start.2 = (bf16[4,1,256]{2,1,0:T(2,128)(2,1)S(1)}, bf16[4,1,256]{2,1,0:T(2,128)(2,1)S(1)}, u32[]{:S(2)}, u32[]{:S(2)}) collective-permute-start(bf16[4,1,256]{2,1,0:T(2,128)(2,1)S(1)} %get-tuple-element.16), channel_id=1, source_target_pairs={{0,1},{2,3},{4,5},{6,7},{8,9},{10,11},{12,13},{14,15},{16,17},{18,... | collective-permute-start | bytes 6152 | tf_op jit(solution)/shard_map/ppermute | solution.py:18
  53.3 3.1 %collective-permute-start.3 = (bf16[4,1,256]{2,1,0:T(2,128)(2,1)S(1)}, bf16[4,1,256]{2,1,0:T(2,128)(2,1)S(1)}, u32[]{:S(2)}, u32[]{:S(2)}) collective-permute-start(bf16[4,1,256]{2,1,0:T(2,128)(2,1)S(1)} %get-tuple-element.15), channel_id=1, source_target_pairs={{1,0},{3,2},{5,4},{7,6},{9,8},{11,10},{13,12},{15,14},{17,16},{19,... | collective-permute-start | bytes 6152 | tf_op jit(solution)/shard_map/ppermute | solution.py:19
  68.9 16.2 %copy-start = (bf16[9,256,512]{2,1,0:T(8,128)(2,1)S(1)}, bf16[9,256,512]{2,1,0:T(8,128)(2,1)}, u32[]{:S(2)}) copy-start(bf16[9,256,512]{2,1,0:T(8,128)(2,1)} %all-gather.4.cloned.1.call-done) | copy-start | bytes 7077892
  71.3 5.0 %collective-permute-start.4 = (bf16[1,64,256]{2,1,0:T(8,128)(2,1)S(1)}, bf16[1,64,256]{2,1,0:T(8,128)(2,1)S(1)}, u32[]{:S(2)}, u32[]{:S(2)}) collective-permute-start(bf16[1,64,256]{2,1,0:T(8,128)(2,1)S(1)} %get-tuple-element.19), channel_id=1, source_target_pairs={{0,2},{2,4},{4,6},{6,8},{8,10},{10,12},{12,14},{1,3},{3,5},{5,7},{... | collective-permute-start | bytes 98312 | tf_op jit(solution)/shard_map/ppermute | solution.py:18
  74.7 5.8 %collective-permute-start.5 = (bf16[1,64,256]{2,1,0:T(8,128)(2,1)S(1)}, bf16[1,64,256]{2,1,0:T(8,128)(2,1)S(1)}, u32[]{:S(2)}, u32[]{:S(2)}) collective-permute-start(bf16[1,64,256]{2,1,0:T(8,128)(2,1)S(1)} %get-tuple-element.20), channel_id=1, source_target_pairs={{2,0},{4,2},{6,4},{8,6},{10,8},{12,10},{14,12},{3,1},{5,3},{7,5},{... | collective-permute-start | bytes 98312 | tf_op jit(solution)/shard_map/ppermute | solution.py:19
  80.5 2.6 %collective-permute-start.6 = (bf16[4,1,256]{2,1,0:T(2,128)(2,1)S(1)}, bf16[4,1,256]{2,1,0:T(2,128)(2,1)S(1)}, u32[]{:S(2)}, u32[]{:S(2)}) collective-permute-start(bf16[4,1,256]{2,1,0:T(2,128)(2,1)S(1)} %get-tuple-element.10), channel_id=1, source_target_pairs={{0,1},{2,3},{4,5},{6,7},{8,9},{10,11},{12,13},{14,15},{16,17},{18,... | collective-permute-start | bytes 6152 | tf_op jit(solution)/shard_map/ppermute | solution.py:18
  81.8 3.1 %collective-permute-start.7 = (bf16[4,1,256]{2,1,0:T(2,128)(2,1)S(1)}, bf16[4,1,256]{2,1,0:T(2,128)(2,1)S(1)}, u32[]{:S(2)}, u32[]{:S(2)}) collective-permute-start(bf16[4,1,256]{2,1,0:T(2,128)(2,1)S(1)} %get-tuple-element.9), channel_id=1, source_target_pairs={{1,0},{3,2},{5,4},{7,6},{9,8},{11,10},{13,12},{15,14},{17,16},{19,... | collective-permute-start | bytes 6152 | tf_op jit(solution)/shard_map/ppermute | solution.py:19
  84.9 6.0 %copy-start.4 = (f32[384]{0:T(512)S(1)}, f32[384]{0:T(512)}, u32[]{:S(2)}) copy-start(f32[384]{0:T(512)} %param.13) | copy-start | bytes 4612
  85.1 40.4 %copy-start.3 = (f32[384]{0:T(512)S(1)}, f32[384]{0:T(512)}, u32[]{:S(2)}) copy-start(f32[384]{0:T(512)} %param.15) | copy-start | bytes 4612
  85.7 3.4 %collective-permute-start.8 = (bf16[2,16,128]{2,1,0:T(8,128)(2,1)S(1)}, bf16[2,16,128]{2,1,0:T(8,128)(2,1)S(1)}, u32[]{:S(2)}, u32[]{:S(2)}) collective-permute-start(bf16[2,16,128]{2,1,0:T(8,128)(2,1)S(1)} %get-tuple-element.22), channel_id=1, source_target_pairs={{0,1},{2,3},{4,5},{6,7},{8,9},{10,11},{12,13},{14,15},{16,17},{18,... | collective-permute-start | bytes 24584 | tf_op jit(solution)/shard_map/ppermute | solution.py:18
  87.8 3.1 %collective-permute-start.9 = (bf16[2,16,128]{2,1,0:T(8,128)(2,1)S(1)}, bf16[2,16,128]{2,1,0:T(8,128)(2,1)S(1)}, u32[]{:S(2)}, u32[]{:S(2)}) collective-permute-start(bf16[2,16,128]{2,1,0:T(8,128)(2,1)S(1)} %get-tuple-element.21), channel_id=1, source_target_pairs={{1,0},{3,2},{5,4},{7,6},{9,8},{11,10},{13,12},{15,14},{17,16},{19,... | collective-permute-start | bytes 24584 | tf_op jit(solution)/shard_map/ppermute | solution.py:19
  91.3 3.4 %collective-permute-start.10 = (bf16[2,32,384]{2,1,0:T(8,128)(2,1)S(1)}, bf16[2,32,384]{2,1,0:T(8,128)(2,1)S(1)}, u32[]{:S(2)}, u32[]{:S(2)}) collective-permute-start(bf16[2,32,384]{2,1,0:T(8,128)(2,1)S(1)} %get-tuple-element.18), channel_id=1, source_target_pairs={{0,1},{2,3},{4,5},{6,7},{8,9},{10,11},{12,13},{14,15},{16,17},{18,... | collective-permute-start | bytes 147464 | tf_op jit(solution)/shard_map/ppermute | solution.py:18
  93.4 3.1 %collective-permute-start.11 = (bf16[2,32,384]{2,1,0:T(8,128)(2,1)S(1)}, bf16[2,32,384]{2,1,0:T(8,128)(2,1)S(1)}, u32[]{:S(2)}, u32[]{:S(2)}) collective-permute-start(bf16[2,32,384]{2,1,0:T(8,128)(2,1)S(1)} %get-tuple-element.17), channel_id=1, source_target_pairs={{1,0},{3,2},{5,4},{7,6},{9,8},{11,10},{13,12},{15,14},{17,16},{19,... | collective-permute-start | bytes 147464 | tf_op jit(solution)/shard_map/ppermute | solution.py:19
  125.5 55.6 %copy-start.2 = (f32[384]{0:T(512)S(1)}, f32[384]{0:T(512)}, u32[]{:S(2)}) copy-start(f32[384]{0:T(512)} %param.17) | copy-start | bytes 4612
  128.0 2.6 %collective-permute-start.12 = (bf16[2,64,384]{2,1,0:T(8,128)(2,1)S(1)}, bf16[2,64,384]{2,1,0:T(8,128)(2,1)S(1)}, u32[]{:S(2)}, u32[]{:S(2)}) collective-permute-start(bf16[2,64,384]{2,1,0:T(8,128)(2,1)S(1)} %fusion.5), channel_id=1, source_target_pairs={{0,1},{2,3},{4,5},{6,7},{8,9},{10,11},{12,13},{14,15},{16,17},{18,... | collective-permute-start | bytes 294920 | tf_op jit(solution)/shard_map/ppermute | solution.py:18
  129.3 3.2 %collective-permute-start.13 = (bf16[2,64,384]{2,1,0:T(8,128)(2,1)S(1)}, bf16[2,64,384]{2,1,0:T(8,128)(2,1)S(1)}, u32[]{:S(2)}, u32[]{:S(2)}) collective-permute-start(bf16[2,64,384]{2,1,0:T(8,128)(2,1)S(1)} %fusion.5), channel_id=1, source_target_pairs={{1,0},{3,2},{5,4},{7,6},{9,8},{11,10},{13,12},{15,14},{17,16},{19,... | collective-permute-start | bytes 294920 | tf_op jit(solution)/shard_map/ppermute | solution.py:19
Sparse Core Ops, SparseCore 0:
  9.5 59.3 all-gather.3
  71.1 54.3 all-gather.5
  127.8 53.3 all-gather.7
where the time goes:
time: 191 us
  waiting for transfers between devices  105 us (55%)
  blocking collectives  36.8 us (19%)
  starting transfers between devices  25.4 us (13%)
  between operations  13.7 us (7%)
  matrix products  8.51 us (4%)
    all_gather x1, waiting for transfers between devices, per_device(): lax.all_gather(third_context_weight, 'rows', axis=1, tiled=True)  48.6 us
    all_gather x1, blocking collectives, per_device(): lax.all_gather(first_context_weight, 'rows', axis=1, tiled=True)  36.8 us
    all_gather x1, waiting for transfers between devices, per_device(): lax.all_gather(second_context_weight, 'rows', axis=1, tiled=True)  29 us
    ppermute x7, starting transfers between devices, extended(): before = lax.ppermute(last, axis, up)  16.3 us
    ppermute x7, waiting for transfers between devices, extended(): after = lax.ppermute(leading, axis, down)  13 us
    all_gather x1, waiting for transfers between devices, per_device(): lax.all_gather(cell_weight, 'rows', axis=1, tiled=True)  12.3 us
    ppermute x7, starting transfers between devices, extended(): after = lax.ppermute(leading, axis, down)  9.04 us
    dot_general x5, matrix products, tap_product(): jnp.dot(flattened, weight.reshape(channels, weight.shape[-1]), preferred_...  8.51 us
  transfers between devices with their start and end apart: 17, of which 10 were waited for; matrix products, arithmetic and copies ran while one was open for 4% of the time, Pallas kernels for 0%

commit v1 on v0

--- a/solution.py
+++ b/solution.py
@@ -6,6 +6,28 @@
 FIRST_DILATION = 16
 SECOND_DILATION = 32
 THIRD_DILATION = 64
+
+
+def in_order(blocks, dim):
+    blocks = jnp.moveaxis(blocks, 0, dim)
+    shape = blocks.shape
+    return blocks.reshape(*shape[:dim], shape[dim] * shape[dim + 1], *shape[dim + 2 :])
+
+
+def collect(value, axis, dim):
+    length = lax.axis_size(axis)
+    pairs = [(i, (i + 1) % length) for i in range(length)]
+    back = [(b, a) for a, b in pairs]
+    lower, upper = ([], [])
+    for step in range(length - 1):
+        if step % 2 == 0:
+            lower.append(lax.ppermute(lower[-1] if lower else value, axis, pairs))
+        else:
+            upper.append(lax.ppermute(upper[-1] if upper else value, axis, back))
+    tiles = jnp.stack([*lower[::-1], value, *upper])
+    shift = lax.axis_index(axis) - len(lower)
+    tiles = tiles[(jnp.arange(length) - shift) % length]
+    return in_order(tiles, dim)
 
 
 def extended(value, sides, width):
@@ -135,7 +157,7 @@
     full_cell, full_first, full_second, full_third = (
         lax.all_gather(cell_weight, "rows", axis=1, tiled=True),
         lax.all_gather(first_context_weight, "rows", axis=1, tiled=True),
-        lax.all_gather(second_context_weight, "rows", axis=1, tiled=True),
+        collect(second_context_weight, "rows", 1),
         lax.all_gather(third_context_weight, "rows", axis=1, tiled=True),
     )
     kernel_list = (full_first, full_second, full_third)

time: 191 us -> 176 us (0.921)
  waiting for transfers between devices: 105 us -> 53.3 us
  starting transfers between devices: 25.4 us -> 40.7 us
  local copies, waits for them, and re-layouts: 1.32 us -> 16.4 us
  blocking collectives: 36.8 us -> 42.9 us
    all_gather x1, waiting for transfers between devices: 48.6 us -> 0.02 us  [per_device(): lax.all_gather(third_context_weight, 'rows', axis=1, tiled=True)]
    ppermute x0 -> x7, waiting for transfers between devices: none -> 41.8 us  [the longest x4 41.8 us: collect(): lower.append(lax.ppermute(lower[-1] if lower else value, axis, pairs))]
    all_gather x1 -> x0, waiting for transfers between devices: 29 us -> none  [per_device(): lax.all_gather(second_context_weight, 'rows', axis=1, tiled=True)]
    ppermute x0 -> x7, starting transfers between devices: none -> 16.3 us  [the longest x3 10.2 us: collect(): upper.append(lax.ppermute(upper[-1] if upper else value, axis, back))]
    all_gather x1, waiting for transfers between devices: 12.3 us -> 0.01 us  [per_device(): lax.all_gather(cell_weight, 'rows', axis=1, tiled=True)]
    unnamed x38 -> x57, local copies, waits for them, and re-layouts: 0.41 us -> 9.92 us
    all_gather x1, blocking collectives: 36.8 us -> 42.9 us  [per_device(): lax.all_gather(first_context_weight, 'rows', axis=1, tiled=True)]
    gather x0 -> x1, local copies, waits for them, and re-layouts: none -> 2.88 us  [collect(): tiles = tiles[(jnp.arange(length) - shift) % length]]
  transfers between devices with their start and end apart: 17 -> 23, of which waited for: 10 -> 9; matrix products, arithmetic and copies ran while one was open for 4% -> 12% of each run, Pallas kernels for 0% -> 0%
where the time goes in v1:
time: 176 us; the launch traced here: 175 us
  waiting for transfers between devices  53.3 us (30%)
  blocking collectives  42.9 us (24%)
  starting transfers between devices  40.7 us (23%)
  local copies, waits for them, and re-layouts  16.4 us (9%)
  between operations  14.1 us (8%)
  matrix products  6.75 us (4%)
    all_gather x1, blocking collectives, per_device(): lax.all_gather(first_context_weight, 'rows', axis=1, tiled=True)  42.9 us
    ppermute x4, waiting for transfers between devices, collect(): lower.append(lax.ppermute(lower[-1] if lower else value, axis, pairs))  41.8 us
    ppermute x7, starting transfers between devices, extended(): before = lax.ppermute(last, axis, up)  15.3 us
    ppermute x7, waiting for transfers between devices, extended(): after = lax.ppermute(leading, axis, down)  10.6 us
    ppermute x3, starting transfers between devices, collect(): upper.append(lax.ppermute(upper[-1] if upper else value, axis, back))  10.2 us
    unnamed x57, local copies, waits for them, and re-layouts  9.92 us
    ppermute x7, starting transfers between devices, extended(): after = lax.ppermute(leading, axis, down)  9.02 us
    dot_general x5, matrix products, tap_product(): jnp.dot(flattened, weight.reshape(channels, weight.shape[-1]), preferred_...  6.75 us
  transfers between devices with their start and end apart: 23, of which 9 were waited for; matrix products, arithmetic and copies ran while one was open for 12% of the time, Pallas kernels for 0%

profile of v1, /device:TPU:0, one launch (start us, length us, event | category | flops | bytes accessed | tf_op | source)
XLA Modules:
  0.0 175.4 jit_solution(29686202189091227)
XLA Ops:
  7.3 3.0 %collective-permute-start.12 = (bf16[9,48,384]{2,1,0:T(8,128)(2,1)}, bf16[9,48,384]{2,1,0:T(8,128)(2,1)}, u32[]{:S(2)}, u32[]{:S(2)}) collective-permute-start(bf16[9,48,384]{2,1,0:T(8,128)(2,1)} %param.14), channel_id=1, source_target_pairs={{0,2},{2,4},{4,6},{6,8},{8,10},{10,12},{12,14},{14,0},{1,3},{3,5},... | collective-permute-start | bytes 995336 | tf_op jit(solution)/shard_map/ppermute | solution.py:24
  10.3 3.1 %collective-permute-start.16 = (bf16[9,48,384]{2,1,0:T(8,128)(2,1)}, bf16[9,48,384]{2,1,0:T(8,128)(2,1)S(1)}, u32[]{:S(2)}, u32[]{:S(2)}) collective-permute-start(bf16[9,48,384]{2,1,0:T(8,128)(2,1)} %param.14), channel_id=1, source_target_pairs={{2,0},{4,2},{6,4},{8,6},{10,8},{12,10},{14,12},{0,14},{3,1},{5,3},... | collective-permute-start | bytes 995336 | tf_op jit(solution)/shard_map/ppermute | solution.py:26
  17.7 42.9 %all_gather.10 = bf16[9,128,384]{2,1,0:T(8,128)(2,1)S(1)} all-gather(bf16[9,16,384]{2,1,0:T(8,128)(2,1)} %param.12), channel_id=1, replica_groups=mesh['segment'=2,'rows'=8,'cols'=2] {'rows'}, dimensions={1}, use_global_device_ids=true | all-gather | bytes 995328 | tf_op jit(solution)/shard_map/all_gather | solution.py:159
  63.3 1.7 collective-permute-done.3
  65.8 16.5 %collective-permute-done.13 = bf16[9,48,384]{2,1,0:T(8,128)(2,1)S(1)} collective-permute-done((bf16[9,48,384]{2,1,0:T(8,128)(2,1)}, bf16[9,48,384]{2,1,0:T(8,128)(2,1)S(1)}, u32[]{:S(2)}, u32[]{:S(2)}) %collective-permute-start.13) | collective-permute-done | bytes 331808 | tf_op jit(solution)/shard_map/ppermute | solution.py:24
  82.5 4.8 %collective-permute-start.17 = (bf16[9,48,384]{2,1,0:T(8,128)(2,1)S(1)}, bf16[9,48,384]{2,1,0:T(8,128)(2,1)}, u32[]{:S(2)}, u32[]{:S(2)}) collective-permute-start(bf16[9,48,384]{2,1,0:T(8,128)(2,1)S(1)} %collective-permute-done.16), channel_id=1, source_target_pairs={{2,0},{4,2},{6,4},{8,6},{10,8},{12,10},{14,12},{0,14},{3,1},{5,3},... | collective-permute-start | bytes 995336 | tf_op jit(solution)/shard_map/ppermute | solution.py:26
  87.2 13.2 %collective-permute-done.14 = bf16[9,48,384]{2,1,0:T(8,128)(2,1)S(1)} collective-permute-done((bf16[9,48,384]{2,1,0:T(8,128)(2,1)S(1)}, bf16[9,48,384]{2,1,0:T(8,128)(2,1)S(1)}, u32[]{:S(2)}, u32[]{:S(2)}) %collective-permute-start.14) | collective-permute-done | bytes 331808 | tf_op jit(solution)/shard_map/ppermute | solution.py:24
  100.4 2.5 %collective-permute-start.15 = (bf16[9,48,384]{2,1,0:T(8,128)(2,1)S(1)}, bf16[9,48,384]{2,1,0:T(8,128)(2,1)S(1)}, u32[]{:S(2)}, u32[]{:S(2)}) collective-permute-start(bf16[9,48,384]{2,1,0:T(8,128)(2,1)S(1)} %collective-permute-done.14), channel_id=1, source_target_pairs={{0,2},{2,4},{4,6},{6,8},{8,10},{10,12},{12,14},{14,0},{1,3},{3,5},... | collective-permute-start | bytes 995336 | tf_op jit(solution)/shard_map/ppermute | solution.py:24
  103.0 2.3 %collective-permute-start.18 = (bf16[9,48,384]{2,1,0:T(8,128)(2,1)}, bf16[9,48,384]{2,1,0:T(8,128)(2,1)}, u32[]{:S(2)}, u32[]{:S(2)}) collective-permute-start(bf16[9,48,384]{2,1,0:T(8,128)(2,1)} %collective-permute-done.17), channel_id=1, source_target_pairs={{2,0},{4,2},{6,4},{8,6},{10,8},{12,10},{14,12},{0,14},{3,1},{5,3},... | collective-permute-start | bytes 995336 | tf_op jit(solution)/shard_map/ppermute | solution.py:26
  105.2 12.0 %collective-permute-done.15 = bf16[9,48,384]{2,1,0:T(8,128)(2,1)S(1)} collective-permute-done((bf16[9,48,384]{2,1,0:T(8,128)(2,1)S(1)}, bf16[9,48,384]{2,1,0:T(8,128)(2,1)S(1)}, u32[]{:S(2)}, u32[]{:S(2)}) %collective-permute-start.15) | collective-permute-done | bytes 331808 | tf_op jit(solution)/shard_map/ppermute | solution.py:24
  119.6 1.7 bitcast_dynamic-update-slice_fusion.4
  121.3 2.3 %convolution_add_fusion.1 = f32[2,64,512]{2,1,0:T(8,128)S(1)} fusion(bf16[2,64,2304]{2,1,0:T(8,128)(2,1)S(1)} %constant_dynamic-update-slice_fusion, bf16[2304,512,1]{1,0,2:T(8,128)(2,1)} %bitcast.49, f32[512]{0:T(512)S(1)} %copy-done.7), kind=kOutput, calls=%fused_computation.2 | convolution fusion | flops 302055424 | bytes 3213312 | tf_op jit(solution)/shard_map/cond/branch_1_fun/dot_general | solution.py:64
  123.7 3.7 %collective-permute-start.4 = (bf16[1,64,256]{2,1,0:T(8,128)(2,1)S(1)}, bf16[1,64,256]{2,1,0:T(8,128)(2,1)S(1)}, u32[]{:S(2)}, u32[]{:S(2)}) collective-permute-start(bf16[1,64,256]{2,1,0:T(8,128)(2,1)S(1)} %get-tuple-element.19), channel_id=1, source_target_pairs={{0,2},{2,4},{4,6},{6,8},{8,10},{10,12},{12,14},{1,3},{3,5},{5,7},{... | collective-permute-start | bytes 98312 | tf_op jit(solution)/shard_map/ppermute | solution.py:40
  129.7 4.3 %collective-permute-done.5 = bf16[1,64,256]{2,1,0:T(8,128)(2,1)S(1)} collective-permute-done((bf16[1,64,256]{2,1,0:T(8,128)(2,1)S(1)}, bf16[1,64,256]{2,1,0:T(8,128)(2,1)S(1)}, u32[]{:S(2)}, u32[]{:S(2)}) %collective-permute-start.5) | collective-permute-done | bytes 32800 | tf_op jit(solution)/shard_map/ppermute | solution.py:41
  136.6 1.8 %bitcast_dynamic-update-slice_fusion.2 = bf16[8,9,48,384]{3,2,1,0:T(8,128)(2,1)} fusion(bf16[8,9,48,384]{3,2,1,0:T(8,128)(2,1)} %bitcast_dynamic-update-slice_fusion.3, bf16[9,48,384]{2,1,0:T(8,128)(2,1)} %copy-done.5), kind=kLoop, calls=%fused_computation.16 | loop fusion | bytes 663552
  139.3 3.0 %collective-permute-start.8 = (bf16[2,16,128]{2,1,0:T(8,128)(2,1)S(1)}, bf16[2,16,128]{2,1,0:T(8,128)(2,1)S(1)}, u32[]{:S(2)}, u32[]{:S(2)}) collective-permute-start(bf16[2,16,128]{2,1,0:T(8,128)(2,1)S(1)} %get-tuple-element.22), channel_id=1, source_target_pairs={{0,1},{2,3},{4,5},{6,7},{8,9},{10,11},{12,13},{14,15},{16,17},{18,... | collective-permute-start | bytes 24584 | tf_op jit(solution)/shard_map/ppermute | solution.py:40
  142.3 1.8 %bitcast_dynamic-update-slice_fusion.1 = bf16[8,9,48,384]{3,2,1,0:T(8,128)(2,1)} fusion(bf16[8,9,48,384]{3,2,1,0:T(8,128)(2,1)} %bitcast_dynamic-update-slice_fusion.2, bf16[9,48,384]{2,1,0:T(8,128)(2,1)} %collective-permute-done.17), kind=kLoop, calls=%fused_computation.15 | loop fusion | bytes 663552
  145.4 1.7 collective-permute-done.9
  148.1 2.7 %collective-permute-start.10 = (bf16[2,32,384]{2,1,0:T(8,128)(2,1)}, bf16[2,32,384]{2,1,0:T(8,128)(2,1)}, u32[]{:S(2)}, u32[]{:S(2)}) collective-permute-start(bf16[2,32,384]{2,1,0:T(8,128)(2,1)} %get-tuple-element.18), channel_id=1, source_target_pairs={{0,1},{2,3},{4,5},{6,7},{8,9},{10,11},{12,13},{14,15},{16,17},{18,... | collective-permute-start | bytes 147464 | tf_op jit(solution)/shard_map/ppermute | solution.py:40
  150.8 1.7 bitcast_dynamic-update-slice_fusion
  152.6 2.9 %gather_fusion = bf16[8,9,48,384]{3,2,1,0:T(8,128)(2,1)S(1)} fusion(bf16[8,9,48,384]{3,2,1,0:T(8,128)(2,1)} %bitcast_dynamic-update-slice_fusion, s32[1024]{0:T(1024)S(1)} %pad_clamp_fusion), kind=kCustom, calls=%fused_computation | custom fusion | bytes 5308448 | tf_op jit(solution)/shard_map/gather | solution.py:29
  160.1 2.1 %collective-permute-start.19 = (bf16[2,64,384]{2,1,0:T(8,128)(2,1)S(1)}, bf16[2,64,384]{2,1,0:T(8,128)(2,1)S(1)}, u32[]{:S(2)}, u32[]{:S(2)}) collective-permute-start(bf16[2,64,384]{2,1,0:T(8,128)(2,1)S(1)} %fusion.5), channel_id=1, source_target_pairs={{0,1},{2,3},{4,5},{6,7},{8,9},{10,11},{12,13},{14,15},{16,17},{18,... | collective-permute-start | bytes 294920 | tf_op jit(solution)/shard_map/ppermute | solution.py:40
  163.6 1.8 %collective-permute-done.20 = bf16[2,64,384]{2,1,0:T(8,128)(2,1)S(1)} collective-permute-done((bf16[2,64,384]{2,1,0:T(8,128)(2,1)S(1)}, bf16[2,64,384]{2,1,0:T(8,128)(2,1)S(1)}, u32[]{:S(2)}, u32[]{:S(2)}) %collective-permute-start.20) | collective-permute-done | bytes 98336 | tf_op jit(solution)/shard_map/ppermute | solution.py:41
  165.5 3.0 %fusion.7 = bf16[1,2,64,384]{3,2,1,0:T(8,128)(2,1)} fusion(bf16[2,64,3456]{2,1,0:T(8,128)(2,1)S(1)} %constant_dynamic-update-slice_fusion.34, bf16[3456,384,1]{1,0,2:T(8,128)(2,1)} %bitcast.52, bf16[2,64,384]{2,1,0:T(8,128)(2,1)S(1)} %fusion.5, f32[384]{0:T(512)S(1)} %copy-done.8), kind=kOutput, calls=%fused_computation.13 | convolution fusion | flops 339984384 | bytes 3737088 | tf_op jit(solution)/shard_map/cond/branch_1_fun/dot_general | solution.py:64
  (117 shorter events, 24.7 us)
Async XLA Ops:
  6.5 114.8 %all-gather.3.cloned.1.call-start = ((), (), s32[]{:S(2)}) async-start(), calls=%async_computation | async-start | bytes 2654208 | tf_op jit(solution)/shard_map/all_gather | solution.py:158
  7.3 158.3 %all-gather.5.cloned.1.call-start = ((), (), s32[]{:S(2)}) async-start(), calls=%async_computation.1 | async-start | bytes 2985984 | tf_op jit(solution)/shard_map/all_gather | solution.py:161
  7.3 57.9 %collective-permute-start.12 = (bf16[9,48,384]{2,1,0:T(8,128)(2,1)}, bf16[9,48,384]{2,1,0:T(8,128)(2,1)}, u32[]{:S(2)}, u32[]{:S(2)}) collective-permute-start(bf16[9,48,384]{2,1,0:T(8,128)(2,1)} %param.14), channel_id=1, source_target_pairs={{0,2},{2,4},{4,6},{6,8},{8,10},{10,12},{12,14},{14,0},{1,3},{3,5},... | collective-permute-start | bytes 995336 | tf_op jit(solution)/shard_map/ppermute | solution.py:24
  10.3 72.1 %collective-permute-start.16 = (bf16[9,48,384]{2,1,0:T(8,128)(2,1)}, bf16[9,48,384]{2,1,0:T(8,128)(2,1)S(1)}, u32[]{:S(2)}, u32[]{:S(2)}) collective-permute-start(bf16[9,48,384]{2,1,0:T(8,128)(2,1)} %param.14), channel_id=1, source_target_pairs={{2,0},{4,2},{6,4},{8,6},{10,8},{12,10},{14,12},{0,14},{3,1},{5,3},... | collective-permute-start | bytes 995336 | tf_op jit(solution)/shard_map/ppermute | solution.py:26
  14.2 46.4 %collective-permute-start = (bf16[1,64,256]{2,1,0:T(8,128)(2,1)S(1)}, bf16[1,64,256]{2,1,0:T(8,128)(2,1)S(1)}, u32[]{:S(2)}, u32[]{:S(2)}) collective-permute-start(bf16[1,64,256]{2,1,0:T(8,128)(2,1)S(1)} %get-tuple-element.23), channel_id=1, source_target_pairs={{0,2},{2,4},{4,6},{6,8},{8,10},{10,12},{12,14},{1,3},{3,5},{5,7},{... | collective-permute-start | bytes 98312 | tf_op jit(solution)/shard_map/ppermute | solution.py:40
  15.5 45.1 %collective-permute-start.1 = (bf16[1,64,256]{2,1,0:T(8,128)(2,1)S(1)}, bf16[1,64,256]{2,1,0:T(8,128)(2,1)S(1)}, u32[]{:S(2)}, u32[]{:S(2)}) collective-permute-start(bf16[1,64,256]{2,1,0:T(8,128)(2,1)S(1)} %get-tuple-element.24), channel_id=1, source_target_pairs={{2,0},{4,2},{6,4},{8,6},{10,8},{12,10},{14,12},{3,1},{5,3},{7,5},{... | collective-permute-start | bytes 98312 | tf_op jit(solution)/shard_map/ppermute | solution.py:41
  17.7 103.6 %copy-start.7 = (f32[512]{0:T(512)S(1)}, f32[512]{0:T(512)}, u32[]{:S(2)}) copy-start(f32[512]{0:T(512)} %param.11) | copy-start | bytes 6148
  60.7 2.6 %collective-permute-start.2 = (bf16[4,1,256]{2,1,0:T(2,128)(2,1)S(1)}, bf16[4,1,256]{2,1,0:T(2,128)(2,1)S(1)}, u32[]{:S(2)}, u32[]{:S(2)}) collective-permute-start(bf16[4,1,256]{2,1,0:T(2,128)(2,1)S(1)} %get-tuple-element.16), channel_id=1, source_target_pairs={{0,1},{2,3},{4,5},{6,7},{8,9},{10,11},{12,13},{14,15},{16,17},{18,... | collective-permute-start | bytes 6152 | tf_op jit(solution)/shard_map/ppermute | solution.py:40
  62.0 3.1 %collective-permute-start.3 = (bf16[4,1,256]{2,1,0:T(2,128)(2,1)S(1)}, bf16[4,1,256]{2,1,0:T(2,128)(2,1)S(1)}, u32[]{:S(2)}, u32[]{:S(2)}) collective-permute-start(bf16[4,1,256]{2,1,0:T(2,128)(2,1)S(1)} %get-tuple-element.15), channel_id=1, source_target_pairs={{1,0},{3,2},{5,4},{7,6},{9,8},{11,10},{13,12},{15,14},{17,16},{19,... | collective-permute-start | bytes 6152 | tf_op jit(solution)/shard_map/ppermute | solution.py:41
  65.2 17.2 %collective-permute-start.13 = (bf16[9,48,384]{2,1,0:T(8,128)(2,1)}, bf16[9,48,384]{2,1,0:T(8,128)(2,1)S(1)}, u32[]{:S(2)}, u32[]{:S(2)}) collective-permute-start(bf16[9,48,384]{2,1,0:T(8,128)(2,1)} %collective-permute-done.12), channel_id=1, source_target_pairs={{0,2},{2,4},{4,6},{6,8},{8,10},{10,12},{12,14},{14,0},{1,3},{3,5},... | collective-permute-start | bytes 995336 | tf_op jit(solution)/shard_map/ppermute | solution.py:24
  82.4 18.0 %collective-permute-start.14 = (bf16[9,48,384]{2,1,0:T(8,128)(2,1)S(1)}, bf16[9,48,384]{2,1,0:T(8,128)(2,1)S(1)}, u32[]{:S(2)}, u32[]{:S(2)}) collective-permute-start(bf16[9,48,384]{2,1,0:T(8,128)(2,1)S(1)} %collective-permute-done.13), channel_id=1, source_target_pairs={{0,2},{2,4},{4,6},{6,8},{8,10},{10,12},{12,14},{14,0},{1,3},{3,5},... | collective-permute-start | bytes 995336 | tf_op jit(solution)/shard_map/ppermute | solution.py:24
  82.5 20.5 %collective-permute-start.17 = (bf16[9,48,384]{2,1,0:T(8,128)(2,1)S(1)}, bf16[9,48,384]{2,1,0:T(8,128)(2,1)}, u32[]{:S(2)}, u32[]{:S(2)}) collective-permute-start(bf16[9,48,384]{2,1,0:T(8,128)(2,1)S(1)} %collective-permute-done.16), channel_id=1, source_target_pairs={{2,0},{4,2},{6,4},{8,6},{10,8},{12,10},{14,12},{0,14},{3,1},{5,3},... | collective-permute-start | bytes 995336 | tf_op jit(solution)/shard_map/ppermute | solution.py:26
  100.4 16.8 %collective-permute-start.15 = (bf16[9,48,384]{2,1,0:T(8,128)(2,1)S(1)}, bf16[9,48,384]{2,1,0:T(8,128)(2,1)S(1)}, u32[]{:S(2)}, u32[]{:S(2)}) collective-permute-start(bf16[9,48,384]{2,1,0:T(8,128)(2,1)S(1)} %collective-permute-done.14), channel_id=1, source_target_pairs={{0,2},{2,4},{4,6},{6,8},{8,10},{10,12},{12,14},{14,0},{1,3},{3,5},... | collective-permute-start | bytes 995336 | tf_op jit(solution)/shard_map/ppermute | solution.py:24
  103.0 47.9 %collective-permute-start.18 = (bf16[9,48,384]{2,1,0:T(8,128)(2,1)}, bf16[9,48,384]{2,1,0:T(8,128)(2,1)}, u32[]{:S(2)}, u32[]{:S(2)}) collective-permute-start(bf16[9,48,384]{2,1,0:T(8,128)(2,1)} %collective-permute-done.17), channel_id=1, source_target_pairs={{2,0},{4,2},{6,4},{8,6},{10,8},{12,10},{14,12},{0,14},{3,1},{5,3},... | collective-permute-start | bytes 995336 | tf_op jit(solution)/shard_map/ppermute | solution.py:26
  123.7 6.0 %collective-permute-start.4 = (bf16[1,64,256]{2,1,0:T(8,128)(2,1)S(1)}, bf16[1,64,256]{2,1,0:T(8,128)(2,1)S(1)}, u32[]{:S(2)}, u32[]{:S(2)}) collective-permute-start(bf16[1,64,256]{2,1,0:T(8,128)(2,1)S(1)} %get-tuple-element.19), channel_id=1, source_target_pairs={{0,2},{2,4},{4,6},{6,8},{8,10},{10,12},{12,14},{1,3},{3,5},{5,7},{... | collective-permute-start | bytes 98312 | tf_op jit(solution)/shard_map/ppermute | solution.py:40
  127.4 6.6 %collective-permute-start.5 = (bf16[1,64,256]{2,1,0:T(8,128)(2,1)S(1)}, bf16[1,64,256]{2,1,0:T(8,128)(2,1)S(1)}, u32[]{:S(2)}, u32[]{:S(2)}) collective-permute-start(bf16[1,64,256]{2,1,0:T(8,128)(2,1)S(1)} %get-tuple-element.20), channel_id=1, source_target_pairs={{2,0},{4,2},{6,4},{8,6},{10,8},{12,10},{14,12},{3,1},{5,3},{7,5},{... | collective-permute-start | bytes 98312 | tf_op jit(solution)/shard_map/ppermute | solution.py:41
  134.0 4.4 %collective-permute-start.6 = (bf16[4,1,256]{2,1,0:T(2,128)(2,1)S(1)}, bf16[4,1,256]{2,1,0:T(2,128)(2,1)S(1)}, u32[]{:S(2)}, u32[]{:S(2)}) collective-permute-start(bf16[4,1,256]{2,1,0:T(2,128)(2,1)S(1)} %get-tuple-element.10), channel_id=1, source_target_pairs={{0,1},{2,3},{4,5},{6,7},{8,9},{10,11},{12,13},{14,15},{16,17},{18,... | collective-permute-start | bytes 6152 | tf_op jit(solution)/shard_map/ppermute | solution.py:40
  135.3 3.1 %collective-permute-start.7 = (bf16[4,1,256]{2,1,0:T(2,128)(2,1)S(1)}, bf16[4,1,256]{2,1,0:T(2,128)(2,1)S(1)}, u32[]{:S(2)}, u32[]{:S(2)}) collective-permute-start(bf16[4,1,256]{2,1,0:T(2,128)(2,1)S(1)} %get-tuple-element.9), channel_id=1, source_target_pairs={{1,0},{3,2},{5,4},{7,6},{9,8},{11,10},{13,12},{15,14},{17,16},{19,... | collective-permute-start | bytes 6152 | tf_op jit(solution)/shard_map/ppermute | solution.py:41
  139.3 6.1 %collective-permute-start.8 = (bf16[2,16,128]{2,1,0:T(8,128)(2,1)S(1)}, bf16[2,16,128]{2,1,0:T(8,128)(2,1)S(1)}, u32[]{:S(2)}, u32[]{:S(2)}) collective-permute-start(bf16[2,16,128]{2,1,0:T(8,128)(2,1)S(1)} %get-tuple-element.22), channel_id=1, source_target_pairs={{0,1},{2,3},{4,5},{6,7},{8,9},{10,11},{12,13},{14,15},{16,17},{18,... | collective-permute-start | bytes 24584 | tf_op jit(solution)/shard_map/ppermute | solution.py:40
  144.0 3.1 %collective-permute-start.9 = (bf16[2,16,128]{2,1,0:T(8,128)(2,1)S(1)}, bf16[2,16,128]{2,1,0:T(8,128)(2,1)S(1)}, u32[]{:S(2)}, u32[]{:S(2)}) collective-permute-start(bf16[2,16,128]{2,1,0:T(8,128)(2,1)S(1)} %get-tuple-element.21), channel_id=1, source_target_pairs={{1,0},{3,2},{5,4},{7,6},{9,8},{11,10},{13,12},{15,14},{17,16},{19,... | collective-permute-start | bytes 24584 | tf_op jit(solution)/shard_map/ppermute | solution.py:41
  148.1 9.4 %collective-permute-start.10 = (bf16[2,32,384]{2,1,0:T(8,128)(2,1)}, bf16[2,32,384]{2,1,0:T(8,128)(2,1)}, u32[]{:S(2)}, u32[]{:S(2)}) collective-permute-start(bf16[2,32,384]{2,1,0:T(8,128)(2,1)} %get-tuple-element.18), channel_id=1, source_target_pairs={{0,1},{2,3},{4,5},{6,7},{8,9},{10,11},{12,13},{14,15},{16,17},{18,... | collective-permute-start | bytes 147464 | tf_op jit(solution)/shard_map/ppermute | solution.py:40
  156.2 3.1 %collective-permute-start.11 = (bf16[2,32,384]{2,1,0:T(8,128)(2,1)S(1)}, bf16[2,32,384]{2,1,0:T(8,128)(2,1)S(1)}, u32[]{:S(2)}, u32[]{:S(2)}) collective-permute-start(bf16[2,32,384]{2,1,0:T(8,128)(2,1)S(1)} %copy-done.6), channel_id=1, source_target_pairs={{1,0},{3,2},{5,4},{7,6},{9,8},{11,10},{13,12},{15,14},{17,16},{19,... | collective-permute-start | bytes 147464 | tf_op jit(solution)/shard_map/ppermute | solution.py:41
  160.1 3.4 %collective-permute-start.19 = (bf16[2,64,384]{2,1,0:T(8,128)(2,1)S(1)}, bf16[2,64,384]{2,1,0:T(8,128)(2,1)S(1)}, u32[]{:S(2)}, u32[]{:S(2)}) collective-permute-start(bf16[2,64,384]{2,1,0:T(8,128)(2,1)S(1)} %fusion.5), channel_id=1, source_target_pairs={{0,1},{2,3},{4,5},{6,7},{8,9},{10,11},{12,13},{14,15},{16,17},{18,... | collective-permute-start | bytes 294920 | tf_op jit(solution)/shard_map/ppermute | solution.py:40
  162.2 3.2 %collective-permute-start.20 = (bf16[2,64,384]{2,1,0:T(8,128)(2,1)S(1)}, bf16[2,64,384]{2,1,0:T(8,128)(2,1)S(1)}, u32[]{:S(2)}, u32[]{:S(2)}) collective-permute-start(bf16[2,64,384]{2,1,0:T(8,128)(2,1)S(1)} %fusion.5), channel_id=1, source_target_pairs={{1,0},{3,2},{5,4},{7,6},{9,8},{11,10},{13,12},{15,14},{17,16},{19,... | collective-permute-start | bytes 294920 | tf_op jit(solution)/shard_map/ppermute | solution.py:41
  (10 other events, 90.5 us)
Sparse Core Ops, SparseCore 0:
  9.5 64.5 all-gather.2
  76.3 70.8 all-gather.4
